TPU v7x, 512 devices: a whole 4x8x8 slice. The times are simulated.
512 devices in a mesh: seq: 128 (over z, y, core), tp: 4 (over x).
Axes of the slice: x: 4, y: 8, z: 8, core: 2. Of those that a mesh axis runs over, the one named last changes fastest.
Arguments:
- tokens: bfloat16 [32768, 1536], P('seq', 'tp'), may hold values from -6 to 6
- norm_gain: float32 [1536], replicated, may hold values from 0.1 to 1.9
- query_weight: bfloat16 [1536, 1536], P(None, 'tp'), may hold values from -0.15625 to 0.15625
- query_bias: float32 [1536], P('tp'), may hold values from -10 to 10
- kv_weight: bfloat16 [1536, 512], P(None, 'tp'), may hold values from -0.15625 to 0.15625
- kv_bias: float32 [512], P('tp'), may hold values from -3 to 3
- out_weight: bfloat16 [1536, 1536], P('tp'), may hold values from -0.625 to 0.625
- shared_slot: bfloat16 [32768, 512], P('seq'), may hold values from -6 to 6
- shared_len: int32 [5], replicated, may hold values from 1 to 256, as said below
- shared_owner: int32 [5], replicated, may hold values from 0 to 127, as said below
- hist_pool: bfloat16 [2048, 64, 512], P('seq'), may hold values from -6 to 6
- hist_pages: int32 [128, 16], P('seq'), may hold values from 0 to 15, each once within a row
- hist_len: int32 [128, 4], P('seq'), may hold values from 1 to 256, as said below
- req_len: int32 [128, 4], P('seq'), may hold values from 1 to 128, 256 in all within a row
- req_offset: int32 [128, 4], P('seq'), may hold values from 0 to 3, each once within a row
- req_parent: int32 [128, 4], P('seq'), may hold values from 0 to 3
Outputs:
- hidden: bfloat16 [32768, 1536], P('seq', 'tp')
- new_cache: bfloat16 [32768, 512], P('seq', 'tp')
Inputs may be any that keep to these rules, and one draw needn't show every extreme that they name: `shared_owner`: all different; entry 0 is the root's. `shared_len`: some entry equals 256. `hist_len`: some request's history has exactly 256 rows.
All inputs are finite; a program needn't handle non-finite values.
Results may differ from a plain program's by a relative error of at most 0.017.
Values may be sent and summed in bfloat16 or wider, within the bound.
No kernel may reach another device: no remote copies, remote signals or barrier semaphores. Data moves between devices by JAX's collectives and lax.ppermute only.
A program may use at most 64 MiB of HBM per device.

v0:
```python
import jax
import jax.numpy as jnp
from jax import lax
from jax.sharding import PartitionSpec as P

norm_eps = 1e-06
rope_base = 1000000.0
neighbour_steps = (-2, -1, 1, 2)
masked_score = -1e30


def from_partner(shard, axis, apart):
    return lax.ppermute(shard, axis, [(i, i ^ 1 << apart) for i in range(lax.axis_size(axis))])


def spread(shard, axis, root):
    mine = lax.axis_index(axis) == root
    return lax.psum(jnp.where(mine, shard, jnp.zeros_like(shard)), axis)


def passed_along(block, axis, distance):
    devices = range(lax.axis_size(axis))
    route = [((i - distance) % len(devices), i) for i in devices]
    return lax.ppermute(block, axis, route)


def request_layout(req_len, req_parent, hist_len, shared_len, row_count):
    request_end = jnp.cumsum(req_len, axis=1)
    request_start = request_end - req_len
    row_index = jnp.arange(row_count, dtype=jnp.int32)
    row_request = jnp.sum(
        (row_index[None, :, None] >= request_end[:, None, :]).astype(jnp.int32), axis=2
    )
    slot_numbers = jnp.arange(req_len.shape[1], dtype=jnp.int32)
    chosen = row_request[:, :, None] == slot_numbers[None, None, :]

    def lookup(table):
        return jnp.sum(jnp.where(chosen, table[:, None, :], 0), axis=2)

    row_offset = row_index[None, :] - lookup(request_start)
    row_parent = lookup(req_parent)
    node_numbers = jnp.arange(shared_len.shape[0] - 1, dtype=jnp.int32)
    parent_length = jnp.sum(
        jnp.where(row_parent[:, :, None] == node_numbers, shared_len[1:], 0), axis=2
    )
    position = shared_len[0] + parent_length + lookup(hist_len) + row_offset
    return (row_request, row_parent, position)


def rotate(values, position):
    half_dim = values.shape[-1] // 2
    frequency = rope_base ** (-2.0 * jnp.arange(half_dim, dtype=jnp.float32) / values.shape[-1])
    angle = position.astype(jnp.float32)[:, None, None] * frequency
    cosine = jnp.cos(angle)
    sine = jnp.sin(angle)
    first_half = values[..., :half_dim]
    second_half = values[..., half_dim:]
    return jnp.concatenate(
        [first_half * cosine - second_half * sine, second_half * cosine + first_half * sine],
        axis=-1,
    )


def partial_attention(queries, key_vectors, value_vectors, key_mask):
    score_scale = queries.shape[-1] ** (-0.5)
    scores = (
        jnp.einsum("rhd,kd->rhk", queries, key_vectors, preferred_element_type=jnp.float32)
        * score_scale
    )
    scores = jnp.where(key_mask[:, None, :], scores, masked_score)
    top_score = jnp.max(scores, axis=2)
    weights = jnp.where(key_mask[:, None, :], jnp.exp(scores - top_score[:, :, None]), 0.0)
    weight_sum = jnp.sum(weights, axis=2)
    mixed = jnp.einsum(
        "rhk,kd->rhd",
        weights.astype(jnp.bfloat16),
        value_vectors,
        preferred_element_type=jnp.float32,
    )
    return (top_score, weight_sum, mixed)


def combine(first_part, second_part):
    top_score = jnp.maximum(first_part[0], second_part[0])
    first_scale = jnp.exp(first_part[0] - top_score)
    second_scale = jnp.exp(second_part[0] - top_score)
    weight_sum = first_part[1] * first_scale + second_part[1] * second_scale
    mixed = first_part[2] * first_scale[:, :, None] + second_part[2] * second_scale[:, :, None]
    return (top_score, weight_sum, mixed)


def on_device(
    tokens,
    norm_gain,
    query_weight,
    query_bias,
    kv_weight,
    kv_bias,
    out_weight,
    shared_slot,
    shared_len,
    shared_owner,
    hist_pool,
    hist_pages,
    hist_len,
    req_len,
    req_offset,
    req_parent,
):
    features = lax.all_gather(tokens, "tp", axis=1, tiled=True)
    widened = features.astype(jnp.float32)
    mean_square = jnp.mean(widened * widened, axis=1, keepdims=True)
    normed = (widened * lax.rsqrt(mean_square + norm_eps) * norm_gain).astype(jnp.bfloat16)
    head_dim = kv_bias.shape[0]
    head_count = query_weight.shape[1] // head_dim
    row_count = features.shape[0]
    tp_index = lax.axis_index("tp")
    kv_group = tp_index // 2
    holds_key = tp_index % 2 == 0
    row_request, row_parent, position = request_layout(
        req_len, req_parent, hist_len, shared_len, row_count
    )
    row_request = row_request[0]
    row_parent = row_parent[0]
    position = position[0]
    queries = jnp.dot(normed, query_weight, preferred_element_type=jnp.float32) + query_bias
    queries = rotate(queries.reshape(row_count, head_count, head_dim), position).astype(
        jnp.bfloat16
    )
    own_block = jnp.dot(normed, kv_weight, preferred_element_type=jnp.float32) + kv_bias
    own_block = jnp.where(
        holds_key, rotate(own_block[:, None, :], position)[:, 0, :], own_block
    ).astype(jnp.bfloat16)
    partner = from_partner(own_block, "tp", 0)
    fresh_keys = jnp.where(holds_key, own_block, partner)
    fresh_values = jnp.where(holds_key, partner, own_block)
    head_columns = lax.dynamic_slice_in_dim(shared_slot, kv_group * 2 * head_dim, 2 * head_dim, 1)
    node_total = shared_owner.shape[0]
    hot_list = [
        spread(head_columns, "seq", shared_owner[level_node]) for level_node in range(node_total)
    ]
    hot_rows = jnp.concatenate(hot_list, axis=0)
    slot_length = head_columns.shape[0]
    hot_node = jnp.repeat(jnp.arange(node_total, dtype=jnp.int32), slot_length)
    hot_place = jnp.tile(jnp.arange(slot_length, dtype=jnp.int32), node_total)
    hot_valid = hot_place < jnp.repeat(shared_len, slot_length)
    every_key = jnp.concatenate([hot_rows[:, :head_dim], fresh_keys], axis=0)
    every_value = jnp.concatenate([hot_rows[:, head_dim:], fresh_values], axis=0)
    block_rows = min(512, row_count)
    row_index = jnp.arange(row_count, dtype=jnp.int32)

    def local_block(block_number):
        row_start = block_number * block_rows
        block_places = row_start + jnp.arange(block_rows, dtype=jnp.int32)
        hot_mask = (
            (hot_node[None, :] == 0) | (hot_node[None, :] == row_parent[:, None] + 1)
        ) & hot_valid[None, :]
        own_mask = (row_request[None, :] == row_request[:, None]) & (
            row_index[None, :] <= block_places[:, None]
        )
        return partial_attention(
            queries, every_key, every_value, jnp.concatenate([hot_mask, own_mask], axis=1)
        )

    local_parts = lax.map(local_block, jnp.arange(row_count // block_rows, dtype=jnp.int32))
    local_parts = tuple((piece.reshape((row_count,) + piece.shape[2:]) for piece in local_parts))
    capacity = row_count // 2
    request_count = req_len.shape[1]
    page_count = hist_pages.shape[1] // request_count
    request_end = jnp.cumsum(req_len[0])
    request_start = request_end - req_len[0]
    padded_queries = jnp.concatenate(
        [queries, jnp.zeros((capacity, head_count, head_dim), jnp.bfloat16)], axis=0
    )
    history_top = jnp.full((row_count + capacity, head_count), masked_score, jnp.float32)
    history_sum = jnp.zeros((row_count + capacity, head_count), jnp.float32)
    history_mix = jnp.zeros((row_count + capacity, head_count, head_dim), jnp.float32)
    capacity_rows = jnp.arange(capacity, dtype=jnp.int32)
    for slot_number in range(request_count):
        offset_step = neighbour_steps[slot_number]
        chosen = req_offset[0] == slot_number
        row_start = jnp.sum(jnp.where(chosen, request_start, 0))
        row_total = jnp.sum(jnp.where(chosen, req_len[0], 0))
        node_depth = jnp.sum(jnp.where(chosen, hist_len[0], 0)).reshape(1)
        window = lax.dynamic_slice_in_dim(padded_queries, row_start, capacity, 0)
        page_rows = hist_pool[
            hist_pages[0, slot_number * page_count : (slot_number + 1) * page_count]
        ]
        flat_pages = page_rows.reshape(-1, page_rows.shape[-1])
        node_places = jnp.arange(flat_pages.shape[0], dtype=jnp.int32)
        node_rows = lax.dynamic_slice_in_dim(flat_pages, kv_group * 2 * head_dim, 2 * head_dim, 1)
        arrived_node = passed_along(node_rows, "seq", -offset_step)
        depth_mask = jnp.broadcast_to(
            (node_places < node_depth[0])[None, :], (capacity, flat_pages.shape[0])
        )
        answer = partial_attention(
            window, arrived_node[:, :head_dim], arrived_node[:, head_dim:], depth_mask
        )
        row_valid = capacity_rows < row_total

        def put_rows(whole_rows, fresh_part):
            region = lax.dynamic_slice_in_dim(whole_rows, row_start, capacity, 0)
            keep_rows = row_valid.reshape((capacity,) + (1,) * (fresh_part.ndim - 1))
            return lax.dynamic_update_slice_in_dim(
                whole_rows, jnp.where(keep_rows, fresh_part, region), row_start, 0
            )

        history_top = put_rows(history_top, answer[0])
        history_sum = put_rows(history_sum, answer[1])
        history_mix = put_rows(history_mix, answer[2])
    history_part = (history_top[:row_count], history_sum[:row_count], history_mix[:row_count])
    merged = combine(local_parts, history_part)
    attention = (
        (merged[2] / merged[1][:, :, None])
        .astype(jnp.bfloat16)
        .reshape(row_count, head_count * head_dim)
    )
    terms = jnp.dot(attention, out_weight, preferred_element_type=jnp.float32)
    summed = lax.psum_scatter(
        terms.astype(jnp.bfloat16), "tp", scatter_dimension=1, tiled=True
    ).astype(jnp.float32)
    hidden = (summed + tokens.astype(jnp.float32)).astype(jnp.bfloat16)
    return (hidden, own_block)


def solution(mesh):
    return jax.shard_map(
        on_device,
        mesh=mesh,
        in_specs=(
            P("seq", "tp"),
            P(),
            P(None, "tp"),
            P("tp"),
            P(None, "tp"),
            P("tp"),
            P("tp", None),
            P("seq", None),
            P(),
            P(),
            P("seq", None, None),
            P("seq", None),
            P("seq", None),
            P("seq", None),
            P("seq", None),
            P("seq", None),
        ),
        out_specs=(P("seq", "tp"), P("seq", "tp")),
        check_vma=False,
    )
```

profile of v0, /device:TPU:8, one launch (start us, length us, event | category | flops | bytes accessed | tf_op | source)
XLA Modules:
  0.0 298.2 jit_solution(13311774897615875516)
XLA Ops:
  8.2 1.8 gather_fusion.1
  10.7 1.9 collective-permute-start.2
  12.7 1.8 gather_fusion.3
  15.1 7.7 %collective-permute-start.4 = (bf16[256,256]{1,0:T(8,128)(2,1)}, bf16[256,256]{1,0:T(8,128)(2,1)}, u32[]{:S(2)}, u32[]{:S(2)}) collective-permute-start(bf16[256,256]{1,0:T(8,128)(2,1)} %constant_dynamic-slice_fusion.4), channel_id=1, source_target_pairs={{8,0},{12,4},{16,8},{20,12},{24,16},{28,20},{32,24},{36,28},{40,32... | collective-permute-start | bytes 393224 | tf_op jit(solution)/shard_map/ppermute | solution.py:24
  22.8 1.8 gather_fusion
  25.3 1.9 collective-permute-start.1
  27.2 1.8 gather_fusion.2
  29.8 7.6 %collective-permute-start.3 = (bf16[256,256]{1,0:T(8,128)(2,1)}, bf16[256,256]{1,0:T(8,128)(2,1)}, u32[]{:S(2)}, u32[]{:S(2)}) collective-permute-start(bf16[256,256]{1,0:T(8,128)(2,1)} %constant_dynamic-slice_fusion.6), channel_id=1, source_target_pairs={{4,0},{8,4},{12,8},{16,12},{20,16},{24,20},{28,24},{32,28},{36,32}... | collective-permute-start | bytes 393224 | tf_op jit(solution)/shard_map/ppermute | solution.py:24
  37.8 14.0 %all_gather.3 = bf16[256,1536]{1,0:T(8,128)(2,1)S(1)} all-gather(bf16[256,384]{1,0:T(8,128)(2,1)S(1)} %copy-done.1), channel_id=1, replica_groups=mesh['seq'=128,'tp'=4] {'tp'}, dimensions={1}, use_global_device_ids=true | all-gather | bytes 983040 | tf_op jit(solution)/shard_map/all_gather | solution.py:110
  53.1 3.1 %collective-permute-start = (bf16[256,128]{0,1:T(8,128)(2,1)S(1)}, bf16[256,128]{0,1:T(8,128)(2,1)}, u32[]{:S(2)}, u32[]{:S(2)}) collective-permute-start(bf16[256,128]{0,1:T(8,128)(2,1)S(1)} %fusion.58), channel_id=1, source_target_pairs={{0,1},{1,0},{2,3},{3,2},{4,5},{5,4},{6,7},{7,6},{8,9},{9,8},{10,11... | collective-permute-start | bytes 196616 | tf_op jit(solution)/shard_map/ppermute | solution.py:13
  69.7 1.3 iota_compare_fusion.7
  71.0 1.2 iota_compare_fusion.6
  75.1 1.9 convolution_add_fusion
  87.0 1.2 fusion.113
  89.3 1.3 dynamic_update_slice.49
  91.6 1.2 fusion.114
  94.8 1.3 dynamic_update_slice.50
  96.4 1.2 fusion.115
  97.6 1.2 convolution_select_fusion
  98.8 1.3 dynamic_update_slice.51
  102.4 151.2 %all-reduce.4.cloned.1.call-done = (bf16[256,256]{1,0:T(8,128)(2,1)}, bf16[256,256]{1,0:T(8,128)(2,1)}, bf16[256,256]{1,0:T(8,128)(2,1)}, bf16[256,256]{1,0:T(8,128)(2,1)}, bf16[256,256]{1,0:T(8,128)(2,1)}) async-done(((bf16[256,256]{1,0:T(8,128)(2,1)}, bf16[256,256]{1,0:T(8,128)(2,1)}, bf16[256,256]{1,0:T(8,128)(2,1)}, bf16[256,256]{1,0:T(8,128)(2,1)}, bf16[256,256]{1,0:T(8,128)(2,1)}), ...) | async-done | bytes 655376 | tf_op jit(solution)/shard_map/psum | solution.py:18
  259.4 1.6 fusion.1
  261.0 1.5 fusion.22
  265.0 24.6 %reduce-scatter.4.cloned.1.call-done = bf16[384,256]{1,0:T(8,128)(2,1)} async-done(((bf16[1536,256]{1,0:T(8,128)(2,1)}), bf16[384,256]{1,0:T(8,128)(2,1)}) %reduce-scatter.4.cloned.1.call-update) | async-done | bytes 196624
  (139 shorter events, 37.3 us)
Async XLA Ops:
  7.2 255.3 %copy-start = (bf16[384,1536]{1,0:T(8,128)(2,1)S(1)}, bf16[384,1536]{1,0:T(8,128)(2,1)}, u32[]{:S(2)}) copy-start(bf16[384,1536]{1,0:T(8,128)(2,1)} %param.22) | copy-start | bytes 3538948
  7.2 30.2 %copy-start.15 = (s32[1,4]{1,0:T(1,128)S(1)}, s32[1,4]{1,0:T(1,128)}, u32[]{:S(2)}) copy-start(s32[1,4]{1,0:T(1,128)} %param.29) | copy-start | bytes 52
  7.2 30.4 %copy-start.13 = (s32[5]{0:T(128)S(1)}, s32[5]{0:T(128)}, u32[]{:S(2)}) copy-start(s32[5]{0:T(128)} %param.24) | copy-start | bytes 64
  7.2 30.6 %copy-start.1 = (bf16[256,384]{1,0:T(8,128)(2,1)S(1)}, bf16[256,384]{1,0:T(8,128)(2,1)}, u32[]{:S(2)}) copy-start(bf16[256,384]{1,0:T(8,128)(2,1)} %param.16) | copy-start | bytes 589828
  7.2 246.4 %all-reduce.4.cloned.1.call-start = ((), (), s32[]{:S(2)}) async-start(), calls=%async_computation.2 | async-start | bytes 1310720 | tf_op jit(solution)/shard_map/psum | solution.py:18
  8.2 43.9 %copy-start.14 = (s32[1,4]{1,0:T(1,128)S(1)}, s32[1,4]{1,0:T(1,128)}, u32[]{:S(2)}) copy-start(s32[1,4]{1,0:T(1,128)} %param.28) | copy-start | bytes 52
  8.2 43.9 %copy-start.17 = (s32[1,4]{1,0:T(1,128)S(1)}, s32[1,4]{1,0:T(1,128)}, u32[]{:S(2)}) copy-start(s32[1,4]{1,0:T(1,128)} %param.31) | copy-start | bytes 52
  10.0 42.3 %copy-start.18 = (bf16[1536,128]{1,0:T(8,128)(2,1)S(1)}, bf16[1536,128]{1,0:T(8,128)(2,1)}, u32[]{:S(2)}) copy-start(bf16[1536,128]{1,0:T(8,128)(2,1)} %param.20) | copy-start | bytes 1179652
  10.0 42.3 %copy-start.19 = (f32[1536]{0:T(1024)S(1)}, f32[1536]{0:T(1024)}, u32[]{:S(2)}) copy-start(f32[1536]{0:T(1024)} %param.17) | copy-start | bytes 18436
  10.0 42.3 %copy-start.21 = (f32[128]{0:T(128)S(1)}, f32[128]{0:T(128)}, u32[]{:S(2)}) copy-start(f32[128]{0:T(128)} %param.21) | copy-start | bytes 1540
  10.7 76.3 %collective-permute-start.2 = (bf16[256,256]{1,0:T(8,128)(2,1)}, bf16[256,256]{1,0:T(8,128)(2,1)}, u32[]{:S(2)}, u32[]{:S(2)}) collective-permute-start(bf16[256,256]{1,0:T(8,128)(2,1)} %constant_dynamic-slice_fusion.8), channel_id=1, source_target_pairs={{508,0},{0,4},{4,8},{8,12},{12,16},{16,20},{20,24},{24,28},{28,32}... | collective-permute-start | bytes 393224 | tf_op jit(solution)/shard_map/ppermute | solution.py:24
  15.1 81.3 %collective-permute-start.4 = (bf16[256,256]{1,0:T(8,128)(2,1)}, bf16[256,256]{1,0:T(8,128)(2,1)}, u32[]{:S(2)}, u32[]{:S(2)}) collective-permute-start(bf16[256,256]{1,0:T(8,128)(2,1)} %constant_dynamic-slice_fusion.4), channel_id=1, source_target_pairs={{8,0},{12,4},{16,8},{20,12},{24,16},{28,20},{32,24},{36,28},{40,32... | collective-permute-start | bytes 393224 | tf_op jit(solution)/shard_map/ppermute | solution.py:24
  25.3 58.4 %collective-permute-start.1 = (bf16[256,256]{1,0:T(8,128)(2,1)}, bf16[256,256]{1,0:T(8,128)(2,1)}, u32[]{:S(2)}, u32[]{:S(2)}) collective-permute-start(bf16[256,256]{1,0:T(8,128)(2,1)} %constant_dynamic-slice_fusion.9), channel_id=1, source_target_pairs={{504,0},{508,4},{0,8},{4,12},{8,16},{12,20},{16,24},{20,28},{24,32... | collective-permute-start | bytes 393224 | tf_op jit(solution)/shard_map/ppermute | solution.py:24
  27.2 29.0 %copy-start.7 = (s32[5]{0:T(128)S(1)}, s32[5]{0:T(128)}, u32[]{:S(2)}) copy-start(s32[5]{0:T(128)} %param.25) | copy-start | bytes 64
  27.2 32.8 %copy-start.6 = (bf16[256,512]{1,0:T(8,128)(2,1)S(1)}, bf16[256,512]{1,0:T(8,128)(2,1)}, u32[]{:S(2)}) copy-start(bf16[256,512]{1,0:T(8,128)(2,1)} %param.23) | copy-start | bytes 786436
  29.8 61.8 %collective-permute-start.3 = (bf16[256,256]{1,0:T(8,128)(2,1)}, bf16[256,256]{1,0:T(8,128)(2,1)}, u32[]{:S(2)}, u32[]{:S(2)}) collective-permute-start(bf16[256,256]{1,0:T(8,128)(2,1)} %constant_dynamic-slice_fusion.6), channel_id=1, source_target_pairs={{4,0},{8,4},{12,8},{16,12},{20,16},{24,20},{28,24},{32,28},{36,32}... | collective-permute-start | bytes 393224 | tf_op jit(solution)/shard_map/ppermute | solution.py:24
  51.8 9.4 %copy-start.16 = (s32[1,4]{1,0:T(1,128)S(1)}, s32[1,4]{1,0:T(1,128)}, u32[]{:S(2)}) copy-start(s32[1,4]{1,0:T(1,128)} %param.30) | copy-start | bytes 52
  51.8 23.3 %copy-start.20 = (f32[384]{0:T(512)S(1)}, f32[384]{0:T(512)}, u32[]{:S(2)}) copy-start(f32[384]{0:T(512)} %param.19) | copy-start | bytes 4612
  53.1 28.2 %copy-start.2 = (bf16[256,128]{0,1:T(8,128)(2,1)}, bf16[256,128]{0,1:T(8,128)(2,1)S(1)}, u32[]{:S(2)}) copy-start(bf16[256,128]{0,1:T(8,128)(2,1)S(1)} %fusion.58) | copy-start | bytes 196612
  53.1 28.2 %collective-permute-start = (bf16[256,128]{0,1:T(8,128)(2,1)S(1)}, bf16[256,128]{0,1:T(8,128)(2,1)}, u32[]{:S(2)}, u32[]{:S(2)}) collective-permute-start(bf16[256,128]{0,1:T(8,128)(2,1)S(1)} %fusion.58), channel_id=1, source_target_pairs={{0,1},{1,0},{2,3},{3,2},{4,5},{5,4},{6,7},{7,6},{8,9},{9,8},{10,11... | collective-permute-start | bytes 196616 | tf_op jit(solution)/shard_map/ppermute | solution.py:13
  60.9 228.6 %reduce-scatter.4.cloned.1.call-start = ((), (), s32[]{:S(2)}) async-start(), calls=%async_computation.1 | async-start | bytes 983040
  91.6 9.5 %copy-start.11 = (pred[128]{0:T(512)(128)(4,1)S(1)}, pred[128]{0:T(512)(128)(4,1)}, u32[]{:S(2)}) copy-start(pred[128]{0:T(512)(128)(4,1)} %iota_compare_fusion.10) | copy-start | bytes 388
  92.8 9.1 %copy-start.10 = (pred[128]{0:T(512)(128)(4,1)S(1)}, pred[128]{0:T(512)(128)(4,1)}, u32[]{:S(2)}) copy-start(pred[128]{0:T(512)(128)(4,1)} %iota_compare_fusion.9) | copy-start | bytes 388
  97.6 160.7 %copy-start.5 = (bf16[256,128]{1,0:T(8,128)(2,1)S(1)}, bf16[256,128]{1,0:T(8,128)(2,1)}, u32[]{:S(2)}) copy-start(bf16[256,128]{1,0:T(8,128)(2,1)} %copy.53) | copy-start | bytes 196612
  (5 other events, 26.5 us)
Sparse Core Ops, SparseCore 0:
  61.1 192.5 all-reduce.3
  264.4 25.1 reduce-scatter.3
where the time goes:
time: 299 us; the launch traced here: 298 us
  waiting for transfers between devices  176 us (59%)
  local copies, waits for them, and re-layouts  26.9 us (9%)
  between operations  25.7 us (9%)
  starting transfers between devices  22.4 us (7%)
  other arithmetic  18.6 us (6%)
  matrix products  14.8 us (5%)
  blocking collectives  14 us (5%)
    psum x1, waiting for transfers between devices, spread(): return lax.psum(jnp.where(mine, shard, jnp.zeros_like(shard)), axis)  151 us
    unnamed x3, waiting for transfers between devices  24.6 us
    ppermute x4, starting transfers between devices, passed_along(): return lax.ppermute(block, axis, route)  19.2 us
    all_gather x1, blocking collectives, on_device(): features = lax.all_gather(tokens, 'tp', axis=1, tiled=True)  14 us
    gather x4, local copies, waits for them, and re-layouts, on_device(): hist_pool[hist_pages[0, slot_number * page_count:(slot_number + 1) * page...  7.21 us
    unnamed x53, local copies, waits for them, and re-layouts  7.08 us
    dynamic_update_slice x12, local copies, waits for them, and re-layouts, put_rows(): lax.dynamic_update_slice_in_dim(whole_rows, jnp.where(keep_rows, fresh_pa...  6.58 us
    dot_general x5, matrix products, partial_attention(): jnp.einsum('rhk,kd->rhd', weights.astype(jnp.bfloat16), value_vectors, pr...  6.09 us
  transfers between devices with their start and end apart: 7, of which 2 were waited for; matrix products, arithmetic and copies ran while one was open for 15% of the time, Pallas kernels for 0%

commit v1 on v0

--- a/solution.py
+++ b/solution.py
@@ -107,7 +107,9 @@
     req_offset,
     req_parent,
 ):
-    features = lax.all_gather(tokens, "tp", axis=1, tiled=True)
+    features = jnp.concatenate(
+        lax.all_to_all(jnp.stack([tokens] * lax.axis_size("tp")), "tp", 0, 0), axis=1
+    )
     widened = features.astype(jnp.float32)
     mean_square = jnp.mean(widened * widened, axis=1, keepdims=True)
     normed = (widened * lax.rsqrt(mean_square + norm_eps) * norm_gain).astype(jnp.bfloat16)

time: 299 us -> 318 us (1.064)
  waiting for transfers between devices: 176 us -> 199 us
  blocking collectives: 14 us -> 0 us
  starting transfers between devices: 22.4 us -> 27.1 us
    psum x1, waiting for transfers between devices: 151 us -> 176 us  [spread(): return lax.psum(jnp.where(mine, shard, jnp.zeros_like(shard)), axis)]
    all_gather x1 -> x0, blocking collectives: 14 us -> none  [on_device(): features = lax.all_gather(tokens, 'tp', axis=1, tiled=True)]
    all_to_all x0 -> x1, starting transfers between devices: none -> 4.42 us  [on_device(): lax.all_to_all(jnp.stack([tokens] * lax.axis_size('tp')), 'tp', 0, 0)]
    unnamed x53 -> x38, local copies, waits for them, and re-layouts: 7.08 us -> 8.09 us
  transfers between devices with their start and end apart: 7 -> 8, of which waited for: 2 -> 2; matrix products, arithmetic and copies ran while one was open for 15% -> 16% of each run, Pallas kernels for 0% -> 0%
where the time goes in v1:
time: 318 us; the launch traced here: 317 us
  waiting for transfers between devices  199 us (63%)
  local copies, waits for them, and re-layouts  28.2 us (9%)
  starting transfers between devices  27.1 us (9%)
  between operations  25.2 us (8%)
  other arithmetic  20.4 us (6%)
  matrix products  16.6 us (5%)
    psum x1, waiting for transfers between devices, spread(): return lax.psum(jnp.where(mine, shard, jnp.zeros_like(shard)), axis)  176 us
    unnamed x3, waiting for transfers between devices  23.6 us
    ppermute x4, starting transfers between devices, passed_along(): return lax.ppermute(block, axis, route)  19.3 us
    unnamed x38, local copies, waits for them, and re-layouts  8.09 us
    gather x4, local copies, waits for them, and re-layouts, on_device(): hist_pool[hist_pages[0, slot_number * page_count:(slot_number + 1) * page...  7.16 us
    dot_general x5, matrix products, partial_attention(): jnp.einsum('rhd,kd->rhk', queries, key_vectors, preferred_element_type=jn...  6.79 us
  transfers between devices with their start and end apart: 8, of which 2 were waited for; matrix products, arithmetic and copies ran while one was open for 16% of the time, Pallas kernels for 0%

profile of v1, /device:TPU:8, one launch (start us, length us, event | category | flops | bytes accessed | tf_op | source)
XLA Modules:
  0.0 317.0 jit_solution(4354307802408616412)
XLA Ops:
  8.1 1.8 gather_fusion.1
  10.6 1.9 collective-permute-start.2
  12.5 1.8 gather_fusion.3
  15.0 7.7 %collective-permute-start.4 = (bf16[256,256]{1,0:T(8,128)(2,1)}, bf16[256,256]{1,0:T(8,128)(2,1)}, u32[]{:S(2)}, u32[]{:S(2)}) collective-permute-start(bf16[256,256]{1,0:T(8,128)(2,1)} %constant_dynamic-slice_fusion.4), channel_id=1, source_target_pairs={{8,0},{12,4},{16,8},{20,12},{24,16},{28,20},{32,24},{36,28},{40,32... | collective-permute-start | bytes 393224 | tf_op jit(solution)/shard_map/ppermute | solution.py:24
  22.7 1.8 gather_fusion
  25.2 1.9 collective-permute-start.1
  27.1 1.8 gather_fusion.2
  29.5 7.8 %collective-permute-start.3 = (bf16[256,256]{1,0:T(8,128)(2,1)}, bf16[256,256]{1,0:T(8,128)(2,1)}, u32[]{:S(2)}, u32[]{:S(2)}) collective-permute-start(bf16[256,256]{1,0:T(8,128)(2,1)} %constant_dynamic-slice_fusion.6), channel_id=1, source_target_pairs={{4,0},{8,4},{12,8},{16,12},{20,16},{24,20},{28,24},{32,28},{36,32}... | collective-permute-start | bytes 393224 | tf_op jit(solution)/shard_map/ppermute | solution.py:24
  39.3 4.4 %all-to-all-start = ((bf16[4,256,384]{1,2,0:T(8,128)(2,1)}), bf16[4,256,384]{1,2,0:T(8,128)(2,1)S(1)}, u32[]{:S(2)}, u32[]{:S(2)}) async-start(bf16[4,256,384]{1,2,0:T(8,128)(2,1)} %stack.2), calls=%async_computation | async-start | bytes 1572864 | tf_op jit(solution)/shard_map/all_to_all | solution.py:111
  59.0 1.2 iota_compare_fusion.11
  63.8 1.2 multiply_cosine_fusion
  66.5 175.8 %all-reduce.4.cloned.1.call-done = (bf16[256,256]{1,0:T(8,128)(2,1)}, bf16[256,256]{1,0:T(8,128)(2,1)}, bf16[256,256]{1,0:T(8,128)(2,1)}, bf16[256,256]{1,0:T(8,128)(2,1)}, bf16[256,256]{1,0:T(8,128)(2,1)}) async-done(((bf16[256,256]{1,0:T(8,128)(2,1)}, bf16[256,256]{1,0:T(8,128)(2,1)}, bf16[256,256]{1,0:T(8,128)(2,1)}, bf16[256,256]{1,0:T(8,128)(2,1)}, bf16[256,256]{1,0:T(8,128)(2,1)}), ...) | async-done | bytes 655376 | tf_op jit(solution)/shard_map/psum | solution.py:18
  248.3 1.9 convolution_add_fusion
  250.4 1.3 convolution_add_fusion.1
  252.1 3.4 %collective-permute-start = (bf16[256,128]{0,1:T(8,128)(2,1)S(1)}, bf16[256,128]{0,1:T(8,128)(2,1)}, u32[]{:S(2)}, u32[]{:S(2)}) collective-permute-start(bf16[256,128]{0,1:T(8,128)(2,1)S(1)} %fusion.55), channel_id=1, source_target_pairs={{0,1},{1,0},{2,3},{3,2},{4,5},{5,4},{6,7},{7,6},{8,9},{9,8},{10,11... | collective-permute-start | bytes 196616 | tf_op jit(solution)/shard_map/ppermute | solution.py:13
  258.4 1.2 fusion.109
  262.0 1.2 fusion.111
  267.7 1.3 dynamic_update_slice.49
  270.1 1.3 dynamic_update_slice.50
  274.6 1.3 dynamic_update_slice.51
  277.0 2.1 fusion
  279.2 1.6 fusion.1
  280.7 1.5 fusion.21
  284.8 23.6 %reduce-scatter.4.cloned.1.call-done = bf16[384,256]{1,0:T(8,128)(2,1)} async-done(((bf16[1536,256]{1,0:T(8,128)(2,1)}), bf16[384,256]{1,0:T(8,128)(2,1)}) %reduce-scatter.4.cloned.1.call-update) | async-done | bytes 196624
  (127 shorter events, 41.1 us)
Async XLA Ops:
  7.2 275.1 %copy-start = (bf16[384,1536]{1,0:T(8,128)(2,1)S(1)}, bf16[384,1536]{1,0:T(8,128)(2,1)}, u32[]{:S(2)}) copy-start(bf16[384,1536]{1,0:T(8,128)(2,1)} %param.22) | copy-start | bytes 3538948
  7.2 36.5 %copy-start.4 = (s32[5]{0:T(128)S(1)}, s32[5]{0:T(128)}, u32[]{:S(2)}) copy-start(s32[5]{0:T(128)} %param.25) | copy-start | bytes 64
  7.2 40.3 %copy-start.3 = (bf16[256,512]{1,0:T(8,128)(2,1)S(1)}, bf16[256,512]{1,0:T(8,128)(2,1)}, u32[]{:S(2)}) copy-start(bf16[256,512]{1,0:T(8,128)(2,1)} %param.23) | copy-start | bytes 786436
  7.2 41.3 %copy-start.8 = (s32[5]{0:T(128)S(1)}, s32[5]{0:T(128)}, u32[]{:S(2)}) copy-start(s32[5]{0:T(128)} %param.24) | copy-start | bytes 64
  7.2 41.4 %copy-start.12 = (s32[1,4]{1,0:T(1,128)S(1)}, s32[1,4]{1,0:T(1,128)}, u32[]{:S(2)}) copy-start(s32[1,4]{1,0:T(1,128)} %param.29) | copy-start | bytes 52
  7.2 41.8 %copy-start.9 = (s32[1,4]{1,0:T(1,128)S(1)}, s32[1,4]{1,0:T(1,128)}, u32[]{:S(2)}) copy-start(s32[1,4]{1,0:T(1,128)} %param.28) | copy-start | bytes 52
  7.2 41.8 %copy-start.11 = (s32[1,4]{1,0:T(1,128)S(1)}, s32[1,4]{1,0:T(1,128)}, u32[]{:S(2)}) copy-start(s32[1,4]{1,0:T(1,128)} %param.30) | copy-start | bytes 52
  7.2 47.8 %copy-start.13 = (s32[1,4]{1,0:T(1,128)S(1)}, s32[1,4]{1,0:T(1,128)}, u32[]{:S(2)}) copy-start(s32[1,4]{1,0:T(1,128)} %param.31) | copy-start | bytes 52
  10.6 246.4 %collective-permute-start.2 = (bf16[256,256]{1,0:T(8,128)(2,1)}, bf16[256,256]{1,0:T(8,128)(2,1)}, u32[]{:S(2)}, u32[]{:S(2)}) collective-permute-start(bf16[256,256]{1,0:T(8,128)(2,1)} %constant_dynamic-slice_fusion.8), channel_id=1, source_target_pairs={{508,0},{0,4},{4,8},{8,12},{12,16},{16,20},{20,24},{24,28},{28,32}... | collective-permute-start | bytes 393224 | tf_op jit(solution)/shard_map/ppermute | solution.py:24
  15.0 256.5 %collective-permute-start.4 = (bf16[256,256]{1,0:T(8,128)(2,1)}, bf16[256,256]{1,0:T(8,128)(2,1)}, u32[]{:S(2)}, u32[]{:S(2)}) collective-permute-start(bf16[256,256]{1,0:T(8,128)(2,1)} %constant_dynamic-slice_fusion.4), channel_id=1, source_target_pairs={{8,0},{12,4},{16,8},{20,12},{24,16},{28,20},{32,24},{36,28},{40,32... | collective-permute-start | bytes 393224 | tf_op jit(solution)/shard_map/ppermute | solution.py:24
  25.2 233.2 %collective-permute-start.1 = (bf16[256,256]{1,0:T(8,128)(2,1)}, bf16[256,256]{1,0:T(8,128)(2,1)}, u32[]{:S(2)}, u32[]{:S(2)}) collective-permute-start(bf16[256,256]{1,0:T(8,128)(2,1)} %constant_dynamic-slice_fusion.9), channel_id=1, source_target_pairs={{504,0},{508,4},{0,8},{4,12},{8,16},{12,20},{16,24},{20,28},{24,32... | collective-permute-start | bytes 393224 | tf_op jit(solution)/shard_map/ppermute | solution.py:24
  29.5 218.5 %copy-start.5 = (f32[1536]{0:T(1024)S(1)}, f32[1536]{0:T(1024)}, u32[]{:S(2)}) copy-start(f32[1536]{0:T(1024)} %param.17) | copy-start | bytes 18436
  29.5 232.5 %collective-permute-start.3 = (bf16[256,256]{1,0:T(8,128)(2,1)}, bf16[256,256]{1,0:T(8,128)(2,1)}, u32[]{:S(2)}, u32[]{:S(2)}) collective-permute-start(bf16[256,256]{1,0:T(8,128)(2,1)} %constant_dynamic-slice_fusion.6), channel_id=1, source_target_pairs={{4,0},{8,4},{12,8},{16,12},{20,16},{24,20},{28,24},{32,28},{36,32}... | collective-permute-start | bytes 393224 | tf_op jit(solution)/shard_map/ppermute | solution.py:24
  39.3 209.0 %copy-start.6 = (f32[384]{0:T(512)S(1)}, f32[384]{0:T(512)}, u32[]{:S(2)}) copy-start(f32[384]{0:T(512)} %param.19) | copy-start | bytes 4612
  39.3 208.5 %all-to-all-start = ((bf16[4,256,384]{1,2,0:T(8,128)(2,1)}), bf16[4,256,384]{1,2,0:T(8,128)(2,1)S(1)}, u32[]{:S(2)}, u32[]{:S(2)}) async-start(bf16[4,256,384]{1,2,0:T(8,128)(2,1)} %stack.2), calls=%async_computation | async-start | bytes 1572864 | tf_op jit(solution)/shard_map/all_to_all | solution.py:111
  43.7 198.6 %all-reduce.4.cloned.1.call-start = ((), (), s32[]{:S(2)}) async-start(), calls=%async_computation.3 | async-start | bytes 1310720 | tf_op jit(solution)/shard_map/psum | solution.py:18
  48.4 260.0 %reduce-scatter.4.cloned.1.call-start = ((), (), s32[]{:S(2)}) async-start(), calls=%async_computation.2 | async-start | bytes 983040
  66.4 184.0 %copy-start.10 = (f32[128]{0:T(128)S(1)}, f32[128]{0:T(128)}, u32[]{:S(2)}) copy-start(f32[128]{0:T(128)} %param.21) | copy-start | bytes 1540
  252.1 23.8 %collective-permute-start = (bf16[256,128]{0,1:T(8,128)(2,1)S(1)}, bf16[256,128]{0,1:T(8,128)(2,1)}, u32[]{:S(2)}, u32[]{:S(2)}) collective-permute-start(bf16[256,128]{0,1:T(8,128)(2,1)S(1)} %fusion.55), channel_id=1, source_target_pairs={{0,1},{1,0},{2,3},{3,2},{4,5},{5,4},{6,7},{7,6},{8,9},{9,8},{10,11... | collective-permute-start | bytes 196616 | tf_op jit(solution)/shard_map/ppermute | solution.py:13
  256.8 16.1 %copy-start.7 = (pred[128]{0:T(512)(128)(4,1)S(1)}, pred[128]{0:T(512)(128)(4,1)}, u32[]{:S(2)}) copy-start(pred[128]{0:T(512)(128)(4,1)} %iota_compare_fusion.9) | copy-start | bytes 388
  277.0 3.7 %copy-start.2 = (bf16[1280,128]{1,0:T(8,128)(2,1)S(1)}, bf16[1280,128]{1,0:T(8,128)(2,1)}, u32[]{:S(2)}) copy-start(bf16[1280,128]{1,0:T(8,128)(2,1)} %get-tuple-element.79) | copy-start | bytes 983044
  282.2 27.2 %copy-start.1 = (bf16[256,384]{1,0:T(8,128)(2,1)S(1)}, bf16[256,384]{1,0:T(8,128)(2,1)}, u32[]{:S(2)}) copy-start(bf16[256,384]{1,0:T(8,128)(2,1)} %param.16) | copy-start | bytes 589828
Sparse Core Ops, SparseCore 0:
  48.5 193.7 all-reduce.3
  284.1 24.1 reduce-scatter.3
